TPU v7x, 32 devices: a whole 2x2x4 slice. The times are simulated.
32 devices in a mesh: teacher: 4 (over y, x), student: 8 (over z, core).
Axes of the slice: x: 2, y: 2, z: 4, core: 2. Of those that a mesh axis runs over, the one named last changes fastest.
Arguments:
- teacher_in: bfloat16 [8192, 8192], P('student', 'teacher')
- teacher_attn: bfloat16 [8192, 4096], P('student', 'teacher'), may hold values from -6 to 6
- teacher_out_proj: bfloat16 [4096, 8192], P('student', 'teacher'), may hold values from -0.09375 to 0.09375
- teacher_gain: bfloat16 [8192], P('teacher'), may hold values from 0.099609375 to 1.8984375
- projection: bfloat16 [8192, 4096], P('teacher', 'student'), may hold values from -0.0625 to 0.0625
- student_in: bfloat16 [8192, 4096], P('student', 'teacher')
- student_attn: bfloat16 [8192, 2048], P('student', 'teacher'), may hold values from -6 to 6
- student_out_proj: bfloat16 [2048, 4096], P('student', 'teacher'), may hold values from -0.125 to 0.125
- student_gain: bfloat16 [4096], P('teacher'), may hold values from 0.099609375 to 1.8984375
- token_ids: int32 [8192], P('student'), may hold values from 0 to 128004, as said below
- row_order: int32 [8192], replicated, may hold values from 0 to 8191, as said below
Outputs:
- grad_weight: float32 [2048, 4096], P('student', 'teacher')
- grad_gain: float32 [4096], P('teacher')
Inputs may be any that keep to these rules, and one draw needn't show every extreme that they name: `token_ids`: within each sequence of 1024 consecutive rows the rows holding 128004 form the sequence's tail, after at least 256 other rows; no other row holds 128004. `row_order`: A permutation of the 8192 rows. For student block k and teacher block b (blocks of 1024 rows), the entries k * 1024 + b * 128 to k * 1024 + (b + 1) * 128 - 1 name rows of teacher block b.
All inputs are finite; a program needn't handle non-finite values.
Results may differ from a plain program's by a relative error of at most 0.02.
Values may be sent and summed in bfloat16 or wider, within the bound.
No kernel may reach another device: no remote copies, remote signals or barrier semaphores. Data moves between devices by JAX's collectives and lax.ppermute only.
A program may use at most 128 MiB of HBM per device.

v0:
```python
import math
import jax
import jax.numpy as jnp
from jax import lax
from jax.sharding import PartitionSpec as P

DT = 8192
DS = 4096
PAD_ID = 128004
epsilon = 1e-05


def shards(
    teacher_in,
    teacher_attn,
    teacher_out_proj,
    teacher_gain,
    projection,
    student_in,
    student_attn,
    student_out_proj,
    student_gain,
    token_ids,
    row_order,
):
    student_count = lax.axis_size("student")
    teacher_count = lax.axis_size("teacher")
    row_count = teacher_in.shape[0]
    piece_rows = row_count // student_count
    student_index = lax.axis_index("student")
    attn_all = lax.all_gather(teacher_attn, "teacher", axis=1, tiled=True)
    columns = attn_all
    branch = jnp.dot(
        columns,
        lax.all_gather(teacher_out_proj, "student", axis=0, tiled=True),
        preferred_element_type=jnp.float32,
    )
    proj_full = lax.all_gather(projection, "student", axis=1, tiled=True)
    residual = teacher_in.astype(jnp.float32) + branch
    square_sum = lax.psum(jnp.sum(residual * residual, axis=1), "teacher")
    teacher_scale = lax.rsqrt(square_sum / DT + epsilon)
    hidden = (residual * teacher_scale[:, None] * teacher_gain.astype(jnp.float32)[None, :]).astype(
        jnp.bfloat16
    )
    proj_blocks = proj_full.reshape(
        proj_full.shape[0], teacher_count, proj_full.shape[1] // teacher_count
    )
    row_blocks = row_order.reshape(student_count, student_count, piece_rows)
    local_rows = (
        lax.dynamic_index_in_dim(row_blocks, student_index, 1, keepdims=False)
        - student_index * row_count
    )
    live_rows = jnp.where(token_ids != PAD_ID, 1.0, 0.0).astype(jnp.bfloat16)
    mask_send = jnp.take(live_rows, local_rows, axis=0)
    columns = proj_blocks
    summed = lax.psum_scatter(
        jnp.einsum("tf,fko->kto", hidden, columns, preferred_element_type=jnp.float32).astype(
            jnp.bfloat16
        ),
        "teacher",
        scatter_dimension=0,
        tiled=True,
    ).astype(jnp.float32)
    target_rows = summed[0].astype(jnp.bfloat16)
    moved, mask_got = (
        lax.all_to_all(
            jnp.take(target_rows, local_rows, axis=0),
            "student",
            split_axis=0,
            concat_axis=0,
            tiled=True,
        ),
        lax.all_to_all(mask_send, "student", split_axis=0, concat_axis=0, tiled=True),
    )
    target = moved.reshape(row_count, moved.shape[2])
    weight_mask = mask_got.reshape(row_count).astype(jnp.float32)
    attn_student = lax.all_gather(student_attn, "teacher", axis=1, tiled=True)
    columns = attn_student
    student_branch = jnp.dot(
        columns,
        lax.all_gather(student_out_proj, "student", axis=0, tiled=True),
        preferred_element_type=jnp.float32,
    )
    student_res = student_in.astype(jnp.float32) + student_branch
    student_square = lax.psum(jnp.sum(student_res * student_res, axis=1), "teacher")
    student_scale = lax.rsqrt(student_square / DS + epsilon)
    normed = student_res * student_scale[:, None]
    gain_values = student_gain.astype(jnp.float32)[None, :]
    distance = normed * gain_values - target.astype(jnp.float32)
    loss_weight = 1.0 / math.sqrt(row_count * student_count)
    grad_out = distance * (weight_mask * loss_weight)[:, None]
    gain_part = jnp.sum(grad_out * normed, axis=0)
    grad_norm = grad_out * gain_values
    inner_sum = lax.psum(jnp.sum(grad_norm * normed, axis=1), "teacher")
    grad_res = (student_scale[:, None] * (grad_norm - normed * (inner_sum / DS)[:, None])).astype(
        jnp.bfloat16
    )
    columns = attn_student
    grad_weight = lax.psum_scatter(
        lax.dot_general(
            columns, grad_res, (((0,), (0,)), ((), ())), preferred_element_type=jnp.float32
        ).astype(jnp.bfloat16),
        "student",
        scatter_dimension=0,
        tiled=True,
    ).astype(jnp.float32)
    grad_gain = lax.psum(gain_part, "student")
    return (grad_weight, grad_gain)


def solution(mesh):
    placed = (
        P("student", "teacher"),
        P("student", "teacher"),
        P("student", "teacher"),
        P("teacher"),
        P("teacher", "student"),
        P("student", "teacher"),
        P("student", "teacher"),
        P("student", "teacher"),
        P("teacher"),
        P("student"),
        P(),
    )
    return jax.shard_map(
        shards,
        mesh=mesh,
        in_specs=placed,
        out_specs=(P("student", "teacher"), P("teacher")),
        check_vma=False,
    )
```

profile of v0, /device:TPU:0, one launch (start us, length us, event | category | flops | bytes accessed | tf_op | source)
XLA Modules:
  0.0 761.1 jit_solution(17488649339242364918)
XLA Ops:
  10.0 2.5 copy.28
  12.6 2.9 copy.27
  15.5 49.5 %all-gather.6.cloned.1.call-done = bf16[1024,2048]{1,0:T(8,128)(2,1)} async-done(((bf16[1024,512]{1,0:T(8,128)(2,1)}), bf16[1024,2048]{1,0:T(8,128)(2,1)}) %all-gather.6.cloned.1.call-update) | async-done | bytes 4194320 | tf_op jit(solution)/shard_map/all_gather | solution.py:77
  65.0 48.5 %all-gather.8.cloned.1.call-done = bf16[2048,1024]{1,0:T(8,128)(2,1)} async-done(((bf16[256,1024]{1,0:T(8,128)(2,1)}), bf16[2048,1024]{1,0:T(8,128)(2,1)}) %all-gather.8.cloned.1.call-update) | async-done | bytes 4194320 | tf_op jit(solution)/shard_map/all_gather | solution.py:81
  113.5 10.3 %multiply_reduce_fusion.3 = (f32[1024]{0:T(1024)S(1)}, f32[1024,1024]{0,1:T(8,128)}) fusion(bf16[1024,2048]{1,0:T(8,128)(2,1)} %all-gather.6.cloned.1.call-done, bf16[2048,1024]{1,0:T(8,128)(2,1)} %all-gather.8.cloned.1.call-done, bf16[1024,1024]{0,1:T(8,128)(2,1)S(1)} %copy.27), kind=kOutput, calls=%fused_computation.16 | convolution fusion | flops 4299160576 | bytes 14684160 | tf_op jit(solution)/shard_map/dot_general | solution.py:79
  123.8 77.9 %all-gather.10.cloned.1.call-done = bf16[1024,4096]{1,0:T(8,128)(2,1)} async-done(((bf16[1024,1024]{1,0:T(8,128)(2,1)}), bf16[1024,4096]{1,0:T(8,128)(2,1)}) %all-gather.10.cloned.1.call-update) | async-done | bytes 8388624 | tf_op jit(solution)/shard_map/all_gather | solution.py:31
  201.7 152.6 %all-gather.12.cloned.1.call-done = bf16[4096,2048]{1,0:T(8,128)(2,1)} async-done(((bf16[512,2048]{1,0:T(8,128)(2,1)}), bf16[4096,2048]{1,0:T(8,128)(2,1)}) %all-gather.12.cloned.1.call-update) | async-done | bytes 16777232 | tf_op jit(solution)/shard_map/all_gather | solution.py:35
  354.2 24.6 %multiply_reduce_fusion = (f32[1024]{0:T(1024)S(1)}, f32[1024,2048]{1,0:T(8,128)}) fusion(bf16[1024,2048]{1,0:T(8,128)(2,1)} %param.11, bf16[1024,4096]{1,0:T(8,128)(2,1)} %all-gather.10.cloned.1.call-done, bf16[4096,2048]{1,0:T(8,128)(2,1)} %all-gather.12.cloned.1.call-done), kind=kOutput, calls=%fused_computation.4 | convolution fusion | flops 17188257792 | bytes 37752832 | tf_op jit(solution)/shard_map/dot_general | solution.py:33
  378.8 10.2 %all-reduce.1 = (f32[1024]{0:T(1024)S(1)}, f32[1024]{0:T(1024)S(1)}) all-reduce(f32[1024]{0:T(1024)S(1)} %get-tuple-element.14, f32[1024]{0:T(1024)S(1)} %get-tuple-element.16), channel_id=1, replica_groups=mesh['teacher'=4,'student'=8] {'teacher'}, use_global_device_ids=true, to_apply=%region_3.4 | all-reduce | flops 2048 | bytes 16384 | tf_op jit(solution)/shard_map/psum | solution.py:40
  389.0 116.0 %all-gather.14.cloned.1.call-done = bf16[2048,4096]{0,1:T(8,128)(2,1)} async-done(((bf16[2048,512]{0,1:T(8,128)(2,1)}), bf16[2048,4096]{0,1:T(8,128)(2,1)}) %all-gather.14.cloned.1.call-update) | async-done | bytes 16777232 | tf_op jit(solution)/shard_map/all_gather | solution.py:38
  505.0 25.5 %convert_bitcast_fusion = bf16[4,1024,1024]{2,1,0:T(8,128)(2,1)} fusion(bf16[2048,4,1024]{0,2,1:T(8,128)(2,1)} %bitcast.51, f32[1024,2048]{1,0:T(8,128)} %get-tuple-element.15, bf16[1024,2048]{1,0:T(8,128)(2,1)} %param.11, f32[2048]{0:T(1024)S(1)} %convert_element_type.58, f32[1024]{0:T(1024)S(1)} %add_rsqrt_fusion), kind=kOutput, calls=%fused_computation.2 | convolution fusion | flops 17194549248 | bytes 37761024 | tf_op jit(solution)/shard_map/tf,fko->kto/dot_general | solution.py:57
  531.3 6.8 gather_fusion.1
  539.5 3.3 all-to-all-start.1
  542.8 72.3 %reduce-scatter.7.cloned.1.call-done = bf16[1,1024,1024]{2,1,0:T(8,128)(2,1)} async-done(((bf16[4,1024,1024]{2,1,0:T(8,128)(2,1)}), bf16[1,1024,1024]{2,1,0:T(8,128)(2,1)}) %reduce-scatter.7.cloned.1.call-update) | async-done | bytes 2097168
  615.2 6.8 gather_fusion
  622.0 2.4 copy.30
  624.4 3.2 broadcast_select_fusion
  627.6 4.6 all-to-all-start
  632.2 48.9 %all-to-all-done = bf16[8,128,1024]{1,2,0:T(8,128)(2,1)S(1)} async-done(((bf16[8,128,1024]{1,2,0:T(8,128)(2,1)}), bf16[8,128,1024]{1,2,0:T(8,128)(2,1)S(1)}, u32[]{:S(2)}, u32[]{:S(2)}) %all-to-all-start) | async-done | bytes 2097184 | tf_op jit(solution)/shard_map/all_to_all | solution.py:66
  681.2 3.5 multiply_reduce_fusion.1
  684.7 9.0 %psum.30 = f32[1024]{0:T(1024)S(1)} all-reduce(f32[1024]{0:T(1024)S(1)} %get-tuple-element.11), channel_id=1, replica_groups=mesh['teacher'=4,'student'=8] {'teacher'}, use_global_device_ids=true, to_apply=%region_6.7 | all-reduce | flops 1024 | bytes 8192 | tf_op jit(solution)/shard_map/psum | solution.py:94
  693.6 10.3 %convert_bitcast_fusion.2 = bf16[2048,1024]{0,1:T(8,128)(2,1)} fusion(bf16[1024,2048]{1,0:T(8,128)(2,1)} %all-gather.6.cloned.1.call-done, f32[1024,1024]{0,1:T(8,128)} %get-tuple-element.17, f32[1024]{0:T(1024)S(1)} %broadcast_multiply_fusion, f32[1024]{0:T(1024)S(1)} %bitcast.47, f32[1024]{0:T(1024)S(1)} %convert_element_type.56, ...), kind=kOutput, calls=%fused_computation.11 | convolution fusion | flops 4307550208 | bytes 14696448 | tf_op jit(solution)/shard_map/dot_general | solution.py:100
  703.9 14.7 %psum.31 = f32[1024]{0:T(1024)} all-reduce(f32[1024]{0:T(1024)S(1)} %get-tuple-element.10), channel_id=1, replica_groups=mesh['teacher'=4,'student'=8] {'student'}, use_global_device_ids=true, to_apply=%region_9.10 | all-reduce | flops 1024 | bytes 8192 | tf_op jit(solution)/shard_map/psum | solution.py:107
  718.6 33.4 %reduce-scatter.5.cloned.1.call-done = bf16[256,1024]{0,1:T(8,128)(2,1)} async-done(((bf16[2048,1024]{0,1:T(8,128)(2,1)}), bf16[256,1024]{0,1:T(8,128)(2,1)}) %reduce-scatter.5.cloned.1.call-update) | async-done | bytes 524304 | tf_op jit(solution)/shard_map/reduce_scatter | solution.py:99
  (35 shorter events, 7.3 us)
Async XLA Ops:
  7.2 2.9 copy-start
  7.2 57.8 %all-gather.6.cloned.1.call-start = ((), (), s32[]{:S(2)}) async-start(), calls=%async_computation.4 | async-start | bytes 5242880 | tf_op jit(solution)/shard_map/all_gather | solution.py:77
  7.9 105.6 %all-gather.8.cloned.1.call-start = ((), (), s32[]{:S(2)}) async-start(), calls=%async_computation.5 | async-start | bytes 4718592 | tf_op jit(solution)/shard_map/all_gather | solution.py:81
  8.7 193.0 %all-gather.10.cloned.1.call-start = ((), (), s32[]{:S(2)}) async-start(), calls=%async_computation.6 | async-start | bytes 10485760 | tf_op jit(solution)/shard_map/all_gather | solution.py:31
  9.4 344.8 %all-gather.12.cloned.1.call-start = ((), (), s32[]{:S(2)}) async-start(), calls=%async_computation.7 | async-start | bytes 18874368 | tf_op jit(solution)/shard_map/all_gather | solution.py:35
  10.0 495.0 %all-gather.14.cloned.1.call-start = ((), (), s32[]{:S(2)}) async-start(), calls=%async_computation.8 | async-start | bytes 18874368 | tf_op jit(solution)/shard_map/all_gather | solution.py:38
  12.6 2.9 copy-start.1
  12.6 602.6 %reduce-scatter.7.cloned.1.call-start = ((), (), s32[]{:S(2)}) async-start(), calls=%async_computation.10 | async-start | bytes 10485760
  530.5 0.8 copy-start.2
  539.5 88.1 %all-to-all-start.1 = ((bf16[8,1,128]{2,1,0:T(2,128)(2,1)}), bf16[8,1,128]{2,1,0:T(2,128)(2,1)S(1)}, u32[]{:S(2)}, u32[]{:S(2)}) async-start(bf16[8,1,128]{2,1,0:T(2,128)(2,1)} %and_select_fusion), calls=%async_computation.1 | async-start | bytes 8192 | tf_op jit(solution)/shard_map/all_to_all | solution.py:73
  624.4 7.8 %copy-start.3 = (bf16[1024]{0:T(1024)(128)(2,1)S(1)}, bf16[1024]{0:T(1024)(128)(2,1)}, u32[]{:S(2)}) copy-start(bf16[1024]{0:T(1024)(128)(2,1)} %param.19) | copy-start | bytes 6148
  627.6 53.6 %all-to-all-start = ((bf16[8,128,1024]{1,2,0:T(8,128)(2,1)}), bf16[8,128,1024]{1,2,0:T(8,128)(2,1)S(1)}, u32[]{:S(2)}, u32[]{:S(2)}) async-start(bf16[8,128,1024]{1,2,0:T(8,128)(2,1)} %broadcast_select_fusion), calls=%async_computation | async-start | bytes 4194304 | tf_op jit(solution)/shard_map/all_to_all | solution.py:66
  632.2 119.9 %reduce-scatter.5.cloned.1.call-start = ((), (), s32[]{:S(2)}) async-start(), calls=%async_computation.9 | async-start | bytes 4718592 | tf_op jit(solution)/shard_map/reduce_scatter | solution.py:99
Sparse Core Ops, SparseCore 0:
  9.8 55.1 all-gather.5
  66.6 46.8 all-gather.7
  115.4 86.2 all-gather.9
  203.1 151.0 all-gather.11
  355.7 149.2 all-gather.13
  530.6 84.5 reduce-scatter.6
  704.0 47.9 reduce-scatter.4
where the time goes:
time: 762 us; the launch traced here: 761 us
  waiting for transfers between devices  602 us (79%)
  matrix products  70.6 us (9%)
  blocking collectives  33.8 us (4%)
  local copies, waits for them, and re-layouts  23.7 us (3%)
  between operations  14.3 us (2%)
  other arithmetic  8.85 us (1%)
  starting transfers between devices  8.17 us (1%)
    all_gather x1, waiting for transfers between devices, shards(): lax.all_gather(teacher_out_proj, 'student', axis=0, tiled=True)  153 us
    all_gather x1, waiting for transfers between devices, shards(): proj_full = lax.all_gather(projection, 'student', axis=1, tiled=True)  116 us
    all_gather x1, waiting for transfers between devices, shards(): attn_all = lax.all_gather(teacher_attn, 'teacher', axis=1, tiled=True)  77.9 us
    unnamed x8, waiting for transfers between devices  75 us
    all_gather x1, waiting for transfers between devices, shards(): attn_student = lax.all_gather(student_attn, 'teacher', axis=1, tiled=True)  49.5 us
    all_to_all x1, waiting for transfers between devices, shards(): lax.all_to_all(jnp.take(target_rows, local_rows, axis=0), 'student', spli...  48.9 us
    all_gather x1, waiting for transfers between devices, shards(): lax.all_gather(student_out_proj, 'student', axis=0, tiled=True)  48.5 us
    reduce_scatter x1, waiting for transfers between devices, shards(): lax.psum_scatter(lax.dot_general(columns, grad_res, (((0,), (0,)), ((), (...  33.4 us
  transfers between devices with their start and end apart: 9, of which 8 were waited for; matrix products, arithmetic and copies ran while one was open for 8% of the time, Pallas kernels for 0%

commit v1 on v0

--- a/solution.py
+++ b/solution.py
@@ -8,6 +8,12 @@
 DS = 4096
 PAD_ID = 128004
 epsilon = 1e-05
+
+
+def laid_out(blocks, dim):
+    lengths = list(blocks.shape[1:])
+    lengths[dim] *= blocks.shape[0]
+    return jnp.moveaxis(blocks, 0, dim).reshape(lengths)
 
 
 def shards(
@@ -74,7 +80,19 @@
     )
     target = moved.reshape(row_count, moved.shape[2])
     weight_mask = mask_got.reshape(row_count).astype(jnp.float32)
-    attn_student = lax.all_gather(student_attn, "teacher", axis=1, tiled=True)
+    size = lax.axis_size("teacher")
+    pairs = [(i, (i + 1) % size) for i in range(size)]
+    back = [(b, a) for a, b in pairs]
+    lower, upper = ([], [])
+    for step in range(size - 1):
+        if step % 2 == 0:
+            lower.append(lax.ppermute(lower[-1] if lower else student_attn, "teacher", pairs))
+        else:
+            upper.append(lax.ppermute(upper[-1] if upper else student_attn, "teacher", back))
+    blocks = jnp.stack([*lower[::-1], student_attn, *upper])
+    shift = lax.axis_index("teacher") - len(lower)
+    blocks = blocks[(jnp.arange(size) - shift) % size]
+    attn_student = laid_out(blocks, 1)
     columns = attn_student
     student_branch = jnp.dot(
         columns,

time: 762 us -> 720 us (0.945)
  waiting for transfers between devices: 602 us -> 539 us
  local copies, waits for them, and re-layouts: 23.7 us -> 32.6 us
    ppermute x0 -> x3, waiting for transfers between devices: none -> 76.5 us  [the longest x2 57.5 us: shards(): lax.ppermute(lower[-1] if lower else student_attn, 'teacher', pairs)]
    all_gather x1 -> x0, waiting for transfers between devices: 49.5 us -> none  [shards(): attn_student = lax.all_gather(student_attn, 'teacher', axis=1, tiled=True)]
    all_gather x1, waiting for transfers between devices: 48.5 us -> 0.01 us  [shards(): lax.all_gather(student_out_proj, 'student', axis=0, tiled=True)]
    all_gather x1, waiting for transfers between devices: 77.9 us -> 36.9 us  [shards(): attn_all = lax.all_gather(teacher_attn, 'teacher', axis=1, tiled=True)]
    unnamed x8 -> x7, waiting for transfers between devices: 75 us -> 74.4 us
  transfers between devices with their start and end apart: 9 -> 11, of which waited for: 8 -> 9; matrix products, arithmetic and copies ran while one was open for 8% -> 11% of each run, Pallas kernels for 0% -> 0%
where the time goes in v1:
time: 720 us
  waiting for transfers between devices  539 us (75%)
  matrix products  72.2 us (10%)
  blocking collectives  33.8 us (5%)
  local copies, waits for them, and re-layouts  32.6 us (5%)
  other arithmetic  14.6 us (2%)
  between operations  14.3 us (2%)
  starting transfers between devices  13.3 us (2%)
    all_gather x1, waiting for transfers between devices, shards(): lax.all_gather(teacher_out_proj, 'student', axis=0, tiled=True)  153 us
    all_gather x1, waiting for transfers between devices, shards(): proj_full = lax.all_gather(projection, 'student', axis=1, tiled=True)  116 us
    unnamed x7, waiting for transfers between devices  74.4 us
    ppermute x2, waiting for transfers between devices, shards(): lax.ppermute(lower[-1] if lower else student_attn, 'teacher', pairs)  57.5 us
    all_to_all x1, waiting for transfers between devices, shards(): lax.all_to_all(jnp.take(target_rows, local_rows, axis=0), 'student', spli...  48.9 us
    all_gather x1, waiting for transfers between devices, shards(): attn_all = lax.all_gather(teacher_attn, 'teacher', axis=1, tiled=True)  36.9 us
    reduce_scatter x1, waiting for transfers between devices, shards(): lax.psum_scatter(lax.dot_general(columns, grad_res, (((0,), (0,)), ((), (...  33.4 us
    dot_general x1, matrix products, shards(): jnp.einsum('tf,fko->kto', hidden, columns, preferred_element_type=jnp.flo...  25.5 us
  transfers between devices with their start and end apart: 11, of which 9 were waited for; matrix products, arithmetic and copies ran while one was open for 11% of the time, Pallas kernels for 0%

profile of v1, /device:TPU:0, one launch (start us, length us, event | category | flops | bytes accessed | tf_op | source)
XLA Modules:
  0.0 719.7 jit_solution(12687186710752636529)
XLA Ops:
  16.0 24.0 %collective-permute-done = bf16[1024,512]{1,0:T(8,128)(2,1)} collective-permute-done((bf16[1024,512]{1,0:T(8,128)(2,1)S(1)}, bf16[1024,512]{1,0:T(8,128)(2,1)}, u32[]{:S(2)}, u32[]{:S(2)}) %collective-permute-start) | collective-permute-done | bytes 1048608 | tf_op jit(solution)/shard_map/ppermute | solution.py:89
  44.1 19.0 %collective-permute-done.2 = bf16[1024,512]{1,0:T(8,128)(2,1)} collective-permute-done((bf16[1024,512]{1,0:T(8,128)(2,1)S(1)}, bf16[1024,512]{1,0:T(8,128)(2,1)}, u32[]{:S(2)}, u32[]{:S(2)}) %collective-permute-start.2) | collective-permute-done | bytes 1048608 | tf_op jit(solution)/shard_map/ppermute | solution.py:91
  63.1 33.5 %collective-permute-done.1 = bf16[1024,512]{1,0:T(8,128)(2,1)} collective-permute-done((bf16[1024,512]{1,0:T(8,128)(2,1)}, bf16[1024,512]{1,0:T(8,128)(2,1)}, u32[]{:S(2)}, u32[]{:S(2)}) %collective-permute-start.1) | collective-permute-done | bytes 1048608 | tf_op jit(solution)/shard_map/ppermute | solution.py:89
  96.6 3.6 pad_maximum_fusion
  100.1 5.0 gather_fusion
  105.1 6.3 copy.25
  111.4 11.6 %multiply_reduce_fusion.3 = (f32[1024]{0:T(1024)S(1)}, f32[1024,1024]{0,1:T(8,128)}) fusion(bf16[1024,2048]{0,1:T(8,128)(2,1)} %bitcast.51, bf16[2048,1024]{1,0:T(8,128)(2,1)} %all-gather.5.cloned.1.call-done, bf16[1024,1024]{0,1:T(8,128)(2,1)S(1)} %copy.26), kind=kOutput, calls=%fused_computation.17 | convolution fusion | flops 4299160576 | bytes 14684160 | tf_op jit(solution)/shard_map/dot_general | solution.py:97
  123.0 36.9 %all-gather.7.cloned.1.call-done = bf16[1024,4096]{1,0:T(8,128)(2,1)} async-done(((bf16[1024,1024]{1,0:T(8,128)(2,1)}), bf16[1024,4096]{1,0:T(8,128)(2,1)}) %all-gather.7.cloned.1.call-update) | async-done | bytes 8388624 | tf_op jit(solution)/shard_map/all_gather | solution.py:37
  159.9 152.7 %all-gather.9.cloned.1.call-done = bf16[4096,2048]{1,0:T(8,128)(2,1)} async-done(((bf16[512,2048]{1,0:T(8,128)(2,1)}), bf16[4096,2048]{1,0:T(8,128)(2,1)}) %all-gather.9.cloned.1.call-update) | async-done | bytes 16777232 | tf_op jit(solution)/shard_map/all_gather | solution.py:41
  312.7 24.6 %multiply_reduce_fusion = (f32[1024]{0:T(1024)S(1)}, f32[1024,2048]{1,0:T(8,128)}) fusion(bf16[1024,2048]{1,0:T(8,128)(2,1)} %param.11, bf16[1024,4096]{1,0:T(8,128)(2,1)} %all-gather.7.cloned.1.call-done, bf16[4096,2048]{1,0:T(8,128)(2,1)} %all-gather.9.cloned.1.call-done), kind=kOutput, calls=%fused_computation.5 | convolution fusion | flops 17188257792 | bytes 37752832 | tf_op jit(solution)/shard_map/dot_general | solution.py:39
  337.3 10.2 %all-reduce.1 = (f32[1024]{0:T(1024)S(1)}, f32[1024]{0:T(1024)S(1)}) all-reduce(f32[1024]{0:T(1024)S(1)} %get-tuple-element.6, f32[1024]{0:T(1024)S(1)} %get-tuple-element.8), channel_id=1, replica_groups=mesh['teacher'=4,'student'=8] {'teacher'}, use_global_device_ids=true, to_apply=%region_3.4 | all-reduce | flops 2048 | bytes 16384 | tf_op jit(solution)/shard_map/psum | solution.py:46
  347.5 115.9 %all-gather.11.cloned.1.call-done = bf16[2048,4096]{0,1:T(8,128)(2,1)} async-done(((bf16[2048,512]{0,1:T(8,128)(2,1)}), bf16[2048,4096]{0,1:T(8,128)(2,1)}) %all-gather.11.cloned.1.call-update) | async-done | bytes 16777232 | tf_op jit(solution)/shard_map/all_gather | solution.py:44
  463.4 25.5 %convert_bitcast_fusion = bf16[4,1024,1024]{2,1,0:T(8,128)(2,1)} fusion(bf16[2048,4,1024]{0,2,1:T(8,128)(2,1)} %bitcast.61, f32[1024,2048]{1,0:T(8,128)} %get-tuple-element.7, bf16[1024,2048]{1,0:T(8,128)(2,1)} %param.11, f32[2048]{0:T(1024)S(1)} %convert_element_type.55, f32[1024]{0:T(1024)S(1)} %add_rsqrt_fusion), kind=kOutput, calls=%fused_computation.3 | convolution fusion | flops 17194549248 | bytes 37761024 | tf_op jit(solution)/shard_map/tf,fko->kto/dot_general | solution.py:63
  489.7 6.8 gather_fusion.2
  497.9 3.3 all-to-all-start.1
  501.2 72.3 %reduce-scatter.7.cloned.1.call-done = bf16[1,1024,1024]{2,1,0:T(8,128)(2,1)} async-done(((bf16[4,1024,1024]{2,1,0:T(8,128)(2,1)}), bf16[1,1024,1024]{2,1,0:T(8,128)(2,1)}) %reduce-scatter.7.cloned.1.call-update) | async-done | bytes 2097168
  573.5 6.8 gather_fusion.1
  585.9 4.6 all-to-all-start
  590.6 48.9 %all-to-all-done = bf16[8,128,1024]{1,2,0:T(8,128)(2,1)S(1)} async-done(((bf16[8,128,1024]{1,2,0:T(8,128)(2,1)}), bf16[8,128,1024]{1,2,0:T(8,128)(2,1)S(1)}, u32[]{:S(2)}, u32[]{:S(2)}) %all-to-all-start) | async-done | bytes 2097184 | tf_op jit(solution)/shard_map/all_to_all | solution.py:72
  639.6 3.5 multiply_reduce_fusion.1
  643.1 8.9 %psum.30 = f32[1024]{0:T(1024)S(1)} all-reduce(f32[1024]{0:T(1024)S(1)} %get-tuple-element.3), channel_id=1, replica_groups=mesh['teacher'=4,'student'=8] {'teacher'}, use_global_device_ids=true, to_apply=%region_6.7 | all-reduce | flops 1024 | bytes 8192 | tf_op jit(solution)/shard_map/psum | solution.py:112
  652.0 10.5 %convolution_convert_fusion = bf16[2048,1024]{1,0:T(8,128)(2,1)} fusion(bf16[1024,2048]{0,1:T(8,128)(2,1)} %bitcast.52, f32[1024,1024]{0,1:T(8,128)} %get-tuple-element.9, f32[1024]{0:T(1024)S(1)} %broadcast_multiply_fusion, f32[1024]{0:T(1024)S(1)} %bitcast.57, f32[1024]{0:T(1024)S(1)} %convert_element_type.53, f32[1024]{0:T(1024)S(1)} %add_rsqrt_fusion.1, ...), kind=kOutput, calls=%fused_computation.19 | convolution fusion | flops 4307550208 | bytes 14696448 | tf_op jit(solution)/shard_map/dot_general | solution.py:118
  662.5 14.7 %psum.31 = f32[1024]{0:T(1024)} all-reduce(f32[1024]{0:T(1024)S(1)} %get-tuple-element.2), channel_id=1, replica_groups=mesh['teacher'=4,'student'=8] {'student'}, use_global_device_ids=true, to_apply=%region_9.10 | all-reduce | flops 1024 | bytes 8192 | tf_op jit(solution)/shard_map/psum | solution.py:125
  677.2 33.4 %reduce-scatter.5.cloned.1.call-done = bf16[256,1024]{1,0:T(8,128)(2,1)} async-done(((bf16[2048,1024]{1,0:T(8,128)(2,1)}), bf16[256,1024]{1,0:T(8,128)(2,1)}) %reduce-scatter.5.cloned.1.call-update) | async-done | bytes 524304 | tf_op jit(solution)/shard_map/reduce_scatter | solution.py:117
  (45 shorter events, 22.7 us)
Async XLA Ops:
  7.2 2.3 copy-start
  7.2 104.2 %all-gather.5.cloned.1.call-start = ((), (), s32[]{:S(2)}) async-start(), calls=%async_computation.4 | async-start | bytes 4718592 | tf_op jit(solution)/shard_map/all_gather | solution.py:99
  7.9 152.0 %all-gather.7.cloned.1.call-start = ((), (), s32[]{:S(2)}) async-start(), calls=%async_computation.5 | async-start | bytes 10485760 | tf_op jit(solution)/shard_map/all_gather | solution.py:37
  8.7 3.3 copy-start.1
  8.7 304.0 %all-gather.9.cloned.1.call-start = ((), (), s32[]{:S(2)}) async-start(), calls=%async_computation.6 | async-start | bytes 18874368 | tf_op jit(solution)/shard_map/all_gather | solution.py:41
  9.4 454.0 %all-gather.11.cloned.1.call-start = ((), (), s32[]{:S(2)}) async-start(), calls=%async_computation.7 | async-start | bytes 18874368 | tf_op jit(solution)/shard_map/all_gather | solution.py:44
  11.9 32.1 %copy-start.2 = (bf16[2048]{0:T(1024)(128)(2,1)S(1)}, bf16[2048]{0:T(1024)(128)(2,1)}, u32[]{:S(2)}) copy-start(bf16[2048]{0:T(1024)(128)(2,1)} %param.14) | copy-start | bytes 12292
  11.9 561.6 %reduce-scatter.7.cloned.1.call-start = ((), (), s32[]{:S(2)}) async-start(), calls=%async_computation.9 | async-start | bytes 10485760
  12.0 28.1 %collective-permute-start = (bf16[1024,512]{1,0:T(8,128)(2,1)S(1)}, bf16[1024,512]{1,0:T(8,128)(2,1)}, u32[]{:S(2)}, u32[]{:S(2)}) collective-permute-start(bf16[1024,512]{1,0:T(8,128)(2,1)S(1)} %copy-done.1), channel_id=1, source_target_pairs={{0,8},{8,16},{16,24},{24,0},{1,9},{9,17},{17,25},{25,1},{2,10},{10... | collective-permute-start | bytes 3145736 | tf_op jit(solution)/shard_map/ppermute | solution.py:89
  15.0 48.1 %collective-permute-start.2 = (bf16[1024,512]{1,0:T(8,128)(2,1)S(1)}, bf16[1024,512]{1,0:T(8,128)(2,1)}, u32[]{:S(2)}, u32[]{:S(2)}) collective-permute-start(bf16[1024,512]{1,0:T(8,128)(2,1)S(1)} %copy-done.1), channel_id=1, source_target_pairs={{8,0},{16,8},{24,16},{0,24},{9,1},{17,9},{25,17},{1,25},{10,2},{18... | collective-permute-start | bytes 3145736 | tf_op jit(solution)/shard_map/ppermute | solution.py:91
  40.1 56.5 %collective-permute-start.1 = (bf16[1024,512]{1,0:T(8,128)(2,1)}, bf16[1024,512]{1,0:T(8,128)(2,1)}, u32[]{:S(2)}, u32[]{:S(2)}) collective-permute-start(bf16[1024,512]{1,0:T(8,128)(2,1)} %collective-permute-done), channel_id=1, source_target_pairs={{0,8},{8,16},{16,24},{24,0},{1,9},{9,17},{17,25},{25,1},{2,10},{10... | collective-permute-start | bytes 3145736 | tf_op jit(solution)/shard_map/ppermute | solution.py:89
  488.9 0.8 copy-start.3
  497.9 88.0 %all-to-all-start.1 = ((bf16[8,1,128]{2,1,0:T(2,128)(2,1)}), bf16[8,1,128]{2,1,0:T(2,128)(2,1)S(1)}, u32[]{:S(2)}, u32[]{:S(2)}) async-start(bf16[8,1,128]{2,1,0:T(2,128)(2,1)} %and_select_fusion), calls=%async_computation.1 | async-start | bytes 8192 | tf_op jit(solution)/shard_map/all_to_all | solution.py:79
  582.8 7.8 %copy-start.4 = (bf16[1024]{0:T(1024)(128)(2,1)S(1)}, bf16[1024]{0:T(1024)(128)(2,1)}, u32[]{:S(2)}) copy-start(bf16[1024]{0:T(1024)(128)(2,1)} %param.19) | copy-start | bytes 6148
  585.9 53.6 %all-to-all-start = ((bf16[8,128,1024]{1,2,0:T(8,128)(2,1)}), bf16[8,128,1024]{1,2,0:T(8,128)(2,1)S(1)}, u32[]{:S(2)}, u32[]{:S(2)}) async-start(bf16[8,128,1024]{1,2,0:T(8,128)(2,1)} %broadcast_select_fusion), calls=%async_computation | async-start | bytes 4194304 | tf_op jit(solution)/shard_map/all_to_all | solution.py:72
  590.5 120.1 %reduce-scatter.5.cloned.1.call-start = ((), (), s32[]{:S(2)}) async-start(), calls=%async_computation.8 | async-start | bytes 4718592 | tf_op jit(solution)/shard_map/reduce_scatter | solution.py:117
Sparse Core Ops, SparseCore 0:
  9.6 49.5 all-gather.4
  61.0 98.8 all-gather.6
  161.5 151.0 all-gather.8
  314.1 149.2 all-gather.10
  489.0 84.4 reduce-scatter.6
  662.6 47.9 reduce-scatter.4
